TPU v7x, 256 devices: a whole 4x4x8 slice. The times are simulated.
256 devices in a mesh: dp: 64 (over z, y, core), mp: 4 (over x).
Axes of the slice: x: 4, y: 4, z: 8, core: 2. Of those that a mesh axis runs over, the one named last changes fastest.
Arguments:
- attention: bfloat16 [8192, 2048], P('dp', 'mp'), may hold values from -6 to 6
- residual: bfloat16 [8192, 2048], P('dp', 'mp'), may hold values from -6 to 6
- out_weight: bfloat16 [2048, 2048], P('mp', 'dp'), may hold values from -0.125 to 0.125
- ffn_gain: float32 [2048], P('mp'), may hold values from 0.1 to 1.9
- shared_gate: bfloat16 [2048, 2816], P('dp', 'mp'), may hold values from -0.125 to 0.125
- shared_up: bfloat16 [2048, 2816], P('dp', 'mp'), may hold values from -0.125 to 0.125
- shared_down: bfloat16 [2816, 2048], P('mp', 'dp'), may hold values from -0.109375 to 0.109375
- expert_gate: bfloat16 [64, 2048, 1408], P('dp', None, 'mp'), may hold values from -0.125 to 0.125
- expert_up: bfloat16 [64, 2048, 1408], P('dp', None, 'mp'), may hold values from -0.125 to 0.125
- expert_down: bfloat16 [64, 1408, 2048], P('dp', 'mp'), may hold values from -0.15625 to 0.15625
- route_ids: int32 [8192, 6], P('dp'), may hold values from 0 to 63, all different within a row; in each aligned block of 128 rows (0 to 127, 128 to 255, ...) at most 16 rows name the same one
- route_scores: float32 [8192, 6], P('dp'), may hold values from 0.05 to 1
- placement: int32 [64], replicated, may hold values from 0 to 63, each once
- next_gain: float32 [2048], P('mp'), may hold values from 0.1 to 1.9
Outputs:
- final: bfloat16 [8192, 2048], P('dp', 'mp')
- next_normed: bfloat16 [8192, 2048], P('dp', 'mp')
Inputs may be any that keep to these rules, and one draw needn't show every extreme that they name: `route_ids`: A token's 6 experts differ. In each aligned block of 128 rows (the rows of one index of dp) no expert is named by more than 16 rows, a bound that some block reaches. `placement`: each storage index is used by exactly one expert.
All inputs are finite; a program needn't handle non-finite values.
Results may differ from a plain program's by a relative error of at most 0.0075.
Values may be sent and summed in bfloat16 or wider, within the bound.
A program may use at most 128 MiB of HBM per device.

v0:
```python
import jax
import jax.numpy as jnp
from jax import lax
from jax.sharding import PartitionSpec as P

D = 2048
EPSILON = 1e-06


def matmul(left, right):
    return jnp.dot(left, right, preferred_element_type=jnp.float32)


def local(
    attention,
    residual,
    out_weight,
    ffn_gain,
    shared_gate,
    shared_up,
    shared_down,
    expert_gate,
    expert_up,
    expert_down,
    route_ids,
    route_scores,
    placement,
    next_gain,
):
    tok_rows = attention.shape[0]
    top_count = route_ids.shape[1]
    experts = lax.axis_size("dp")
    capacity = min(tok_rows, 8 * tok_rows // experts)
    model_width = D
    partial_value = matmul(attention, lax.all_gather(out_weight, "dp", axis=1, tiled=True))
    projected = lax.psum_scatter(partial_value, "mp", scatter_dimension=1, tiled=True)
    hidden = (residual.astype(jnp.float32) + projected).astype(jnp.bfloat16)
    hidden_float = hidden.astype(jnp.float32)
    squares = lax.psum(jnp.sum(hidden_float * hidden_float, axis=1), "mp")
    normed = (hidden_float * lax.rsqrt(squares / model_width + EPSILON)[:, None] * ffn_gain).astype(
        jnp.bfloat16
    )
    whole_rows = lax.all_gather(normed, "mp", axis=1, tiled=True)
    flat_ids = route_ids.reshape(-1)
    expert_iota = jnp.arange(experts, dtype=jnp.int32)
    one_hot = (flat_ids[:, None] == expert_iota[None, :]).astype(jnp.int32)
    target = jnp.sum(one_hot * placement[None, :], axis=1)
    slot = jnp.sum((jnp.cumsum(one_hot, axis=0) - one_hot) * one_hot, axis=1)
    dest = target * capacity + slot
    slots = experts * capacity
    hit = (dest[:, None] == jnp.arange(slots, dtype=jnp.int32)[None, :]).reshape(
        tok_rows, top_count, slots
    )
    flat_scores = route_scores.reshape(tok_rows, top_count)
    combine = jnp.sum(jnp.where(hit, flat_scores[:, :, None], 0.0), axis=1)
    pick = jnp.any(hit, axis=1).astype(jnp.bfloat16)
    outgoing = matmul(pick.T, whole_rows).astype(jnp.bfloat16)
    arrived = lax.all_to_all(
        outgoing.reshape(experts, capacity, model_width),
        "dp",
        split_axis=0,
        concat_axis=0,
        tiled=True,
    )
    in_rows = arrived.reshape(slots, model_width)
    gate_val = matmul(in_rows, expert_gate[0])
    up_val = matmul(in_rows, expert_up[0])
    activated = (jax.nn.silu(gate_val) * up_val).astype(jnp.bfloat16)
    partial_out = matmul(activated, expert_down[0]).astype(jnp.bfloat16)
    returned = lax.all_to_all(
        partial_out.reshape(experts, capacity, model_width),
        "dp",
        split_axis=0,
        concat_axis=0,
        tiled=True,
    ).reshape(slots, model_width)
    routed = jnp.dot(
        combine,
        returned.astype(jnp.float32),
        precision=lax.Precision.HIGHEST,
        preferred_element_type=jnp.float32,
    )
    pieces = (
        lax.all_gather(shared_gate, "dp", axis=0, tiled=True),
        lax.all_gather(shared_up, "dp", axis=0, tiled=True),
    )
    shared_gval = matmul(whole_rows, pieces[0])
    shared_uval = matmul(whole_rows, pieces[1])
    shared_act = (jax.nn.silu(shared_gval) * shared_uval).astype(jnp.bfloat16)
    shared_part = matmul(shared_act, lax.all_gather(shared_down, "dp", axis=1, tiled=True))
    mixture = lax.psum_scatter(routed + shared_part, "mp", scatter_dimension=1, tiled=True)
    final = (hidden_float + mixture).astype(jnp.bfloat16)
    final_float = final.astype(jnp.float32)
    final_squares = lax.psum(jnp.sum(final_float * final_float, axis=1), "mp")
    next_normed = (
        final_float * lax.rsqrt(final_squares / model_width + EPSILON)[:, None] * next_gain
    ).astype(jnp.bfloat16)
    return (final, next_normed)


def solution(mesh):
    in_specs = (
        P("dp", "mp"),
        P("dp", "mp"),
        P("mp", "dp"),
        P("mp"),
        P("dp", "mp"),
        P("dp", "mp"),
        P("mp", "dp"),
        P("dp", None, "mp"),
        P("dp", None, "mp"),
        P("dp", "mp", None),
        P("dp", None),
        P("dp", None),
        P(),
        P("mp"),
    )
    out_specs = (P("dp", "mp"), P("dp", "mp"))
    return jax.shard_map(local, mesh=mesh, in_specs=in_specs, out_specs=out_specs, check_vma=False)
```

profile of v0, /device:TPU:8, one launch (start us, length us, event | category | flops | bytes accessed | tf_op | source)
XLA Modules:
  0.0 476.1 jit_solution(9288351023330188056)
XLA Ops:
  7.2 0.0 copy-start
  7.2 0.0 copy-start.6
  7.2 0.0 copy-start.9
  7.2 0.0 copy-start.4
  7.2 0.0 all-gather.5.cloned.1.call-start
  7.3 0.7 all-gather.5.cloned.1.call-update
  7.9 0.0 copy-start.7
  8.0 0.0 reduce-scatter.3.cloned.1.call-start
  8.0 82.0 %all-gather.5.cloned.1.call-done = bf16[512,2048]{0,1:T(8,128)(2,1)} async-done(((bf16[512,32]{0,1:T(8,128)(2,1)}), bf16[512,2048]{0,1:T(8,128)(2,1)}) %all-gather.5.cloned.1.call-update) | async-done | bytes 2097168 | tf_op jit(solution)/shard_map/all_gather | solution.py:35
  90.0 3.5 fusion.32
  93.5 0.0 reduce-scatter.3.cloned.1.call-update
  93.5 0.0 copy-done.6
  93.5 0.1 copy.21
  93.6 0.1 eq.43
  93.8 0.1 eq.39
  93.9 1.8 reduce-window.6
  95.7 0.3 slice_reduce_fusion
  96.0 0.0 copy-done.9
  96.1 0.1 select_reduce_fusion.1
  96.2 0.1 add.43
  96.4 0.1 copy.24
  96.4 0.5 fusion
  96.9 21.4 %reduce-scatter.3.cloned.1.call-done = f32[128,512]{1,0:T(8,128)} async-done(((f32[128,2048]{1,0:T(8,128)}), f32[128,512]{1,0:T(8,128)}) %reduce-scatter.3.cloned.1.call-update) | async-done | bytes 262160 | tf_op jit(solution)/shard_map/reduce_scatter | solution.py:36
  118.4 0.0 copy-done.4
  118.4 1.1 fusion.20
  119.5 8.5 %psum.14 = f32[128]{0:T(128)S(1)} all-reduce(f32[128]{0:T(128)S(1)} %get-tuple-element.6), channel_id=1, replica_groups=mesh['dp'=64,'mp'=4] {'mp'}, use_global_device_ids=true, to_apply=%region_8.9 | all-reduce | flops 128 | bytes 1024 | tf_op jit(solution)/shard_map/psum | solution.py:39
  128.0 0.0 copy-done.1
  128.0 0.0 copy-done.7
  128.0 0.1 fusion.22
  128.1 13.2 %all_gather.16 = bf16[128,2048]{1,0:T(8,128)(2,1)S(1)} all-gather(bf16[128,512]{1,0:T(8,128)(2,1)S(1)} %fusion.22), channel_id=1, replica_groups=mesh['dp'=64,'mp'=4] {'mp'}, dimensions={1}, use_global_device_ids=true | all-gather | bytes 655360 | tf_op jit(solution)/shard_map/all_gather | solution.py:43
  141.3 3.2 convolution_convert_fusion.1
  144.6 10.6 %all-to-all-start = ((bf16[64,16,2048]{2,1,0:T(8,128)(2,1)}), bf16[64,16,2048]{2,1,0:T(8,128)(2,1)}, u32[]{:S(2)}, u32[]{:S(2)}) async-start(bf16[64,16,2048]{2,1,0:T(8,128)(2,1)} %bitcast.50), calls=%async_computation.1 | async-start | bytes 8388608 | tf_op jit(solution)/shard_map/all_to_all | solution.py:58
  155.2 0.0 all-gather.7.cloned.1.call-start
  155.2 0.7 all-gather.7.cloned.1.call-update
  155.9 0.0 all-gather.11.cloned.1.call-start
  156.0 0.5 all-gather.11.cloned.1.call-update
  156.5 104.0 %all-to-all-done = bf16[64,16,2048]{2,1,0:T(8,128)(2,1)} async-done(((bf16[64,16,2048]{2,1,0:T(8,128)(2,1)}), bf16[64,16,2048]{2,1,0:T(8,128)(2,1)}, u32[]{:S(2)}, u32[]{:S(2)}) %all-to-all-start) | async-done | bytes 4194336 | tf_op jit(solution)/shard_map/all_to_all | solution.py:58
  260.5 0.0 copy-done.10
  260.5 5.1 %fusion.3 = f32[1024,352]{0,1:T(8,128)} fusion(bf16[1024,2048]{1,0:T(8,128)(2,1)} %bitcast.2, bf16[1,2048,352]{1,2,0:T(8,128)(2,1)S(1)} %copy-done.10), kind=kOutput, calls=%fused_computation.9 | convolution fusion | flops 1476395008 | bytes 7077888 | tf_op jit(solution)/shard_map/dot_general | solution.py:11
  265.6 0.0 copy-done
  265.6 8.9 %convolution_convert_fusion = bf16[1024,2048]{1,0:T(8,128)(2,1)} fusion(bf16[1,352,2048]{2,1,0:T(8,128)(2,1)S(1)} %copy-done, bf16[1024,2048]{1,0:T(8,128)(2,1)} %bitcast.2, bf16[1,2048,352]{1,2,0:T(8,128)(2,1)} %param.22, f32[1024,352]{0,1:T(8,128)} %fusion.3), kind=kOutput, calls=%fused_computation | convolution fusion | flops 2957049856 | bytes 12713984 | tf_op jit(solution)/shard_map/dot_general | solution.py:11
  274.6 5.8 %all-to-all-start.1 = ((bf16[64,16,2048]{2,1,0:T(8,128)(2,1)}), bf16[64,16,2048]{2,1,0:T(8,128)(2,1)}, u32[]{:S(2)}, u32[]{:S(2)}) async-start(bf16[64,16,2048]{2,1,0:T(8,128)(2,1)} %bitcast.51), calls=%async_computation.2 | async-start | bytes 8388608 | tf_op jit(solution)/shard_map/all_to_all | solution.py:70
  280.4 0.0 all-gather.9.cloned.1.call-start
  280.4 0.5 all-gather.9.cloned.1.call-update
  281.0 0.2 reduce-scatter.5.cloned.1.call-start
  281.2 0.0 copy-done.5
  281.2 0.4 select_reduce_fusion
  281.6 0.0 all-gather.7.cloned.1.call-done
  281.7 3.9 fusion.34
  285.6 98.6 %all-to-all-done.1 = bf16[64,16,2048]{2,1,0:T(8,128)(2,1)} async-done(((bf16[64,16,2048]{2,1,0:T(8,128)(2,1)}), bf16[64,16,2048]{2,1,0:T(8,128)(2,1)}, u32[]{:S(2)}, u32[]{:S(2)}) %all-to-all-start.1) | async-done | bytes 4194336 | tf_op jit(solution)/shard_map/all_to_all | solution.py:70
  384.2 4.0 fusion.33
  388.2 0.0 copy-start.2
  388.2 0.0 copy-start.8
  388.3 0.0 all-gather.11.cloned.1.call-done
  388.3 38.4 %all-gather.9.cloned.1.call-done = bf16[2048,704]{1,0:T(8,128)(2,1)} async-done(((bf16[32,704]{1,0:T(8,128)(2,1)}), bf16[2048,704]{1,0:T(8,128)(2,1)}) %all-gather.9.cloned.1.call-update) | async-done | bytes 2883600 | tf_op jit(solution)/shard_map/all_gather | solution.py:85
  426.7 7.3 %convolution_add_fusion = f32[128,2048]{1,0:T(8,128)} fusion(f32[128,2048]{1,0:T(8,128)S(1)} %fusion.33, bf16[704,2048]{0,1:T(8,128)(2,1)} %all-gather.11.cloned.1.call-done, bf16[128,2048]{1,0:T(8,128)(2,1)S(1)} %all_gather.16, bf16[2048,704]{1,0:T(8,128)(2,1)} %all-gather.9.cloned.1.call-done, f32[128,704]{0,1:T(8,128)} %fusion.34), kind=kOutput, calls=%fused_computation.5 | convolution fusion | flops 739000320 | bytes 8749056 | tf_op jit(solution)/shard_map/dot_general | solution.py:11
  434.0 0.0 reduce-scatter.5.cloned.1.call-update
  434.0 24.9 %reduce-scatter.5.cloned.1.call-done = f32[128,512]{1,0:T(8,128)} async-done(((f32[128,2048]{1,0:T(8,128)}), f32[128,512]{1,0:T(8,128)}) %reduce-scatter.5.cloned.1.call-update) | async-done | bytes 262160 | tf_op jit(solution)/shard_map/reduce_scatter | solution.py:91
  458.9 0.0 copy-done.2
  458.9 1.1 fusion.17
  460.0 8.5 %psum.15 = f32[128]{0:T(128)S(1)} all-reduce(f32[128]{0:T(128)S(1)} %get-tuple-element.4), channel_id=1, replica_groups=mesh['dp'=64,'mp'=4] {'mp'}, use_global_device_ids=true, to_apply=%region_11.12 | all-reduce | flops 128 | bytes 1024 | tf_op jit(solution)/shard_map/psum | solution.py:94
  468.5 0.0 copy-done.8
  468.5 0.8 fusion.19
  469.3 0.0 copy-done.3
  (9 shorter events, 0.1 us)
Async XLA Ops:
  7.2 258.5 %copy-start = (bf16[1,352,2048]{2,1,0:T(8,128)(2,1)S(1)}, bf16[1,352,2048]{2,1,0:T(8,128)(2,1)}, u32[]{:S(2)}) copy-start(bf16[1,352,2048]{2,1,0:T(8,128)(2,1)} %param.23) | copy-start | bytes 4325380
  7.2 86.3 %copy-start.6 = (s32[128,6]{0,1:T(8,128)S(1)}, s32[128,6]{0,1:T(8,128)}, u32[]{:S(2)}) copy-start(s32[128,6]{0,1:T(8,128)} %param.24) | copy-start | bytes 9220
  7.2 88.9 %copy-start.9 = (s32[64]{0:T(128)S(1)}, s32[64]{0:T(128)}, u32[]{:S(2)}) copy-start(s32[64]{0:T(128)} %param.26) | copy-start | bytes 772
  7.2 111.2 %copy-start.4 = (bf16[128,512]{1,0:T(8,128)(2,1)S(1)}, bf16[128,512]{1,0:T(8,128)(2,1)}, u32[]{:S(2)}) copy-start(bf16[128,512]{1,0:T(8,128)(2,1)} %param.15) | copy-start | bytes 393220
  7.2 82.8 %all-gather.5.cloned.1.call-start = ((), (), s32[]{:S(2)}) async-start(), calls=%async_computation.4 | async-start | bytes 2129920 | tf_op jit(solution)/shard_map/all_gather | solution.py:35
  7.9 120.1 %copy-start.7 = (f32[512]{0:T(512)S(1)}, f32[512]{0:T(512)}, u32[]{:S(2)}) copy-start(f32[512]{0:T(512)} %param.17) | copy-start | bytes 6148
  8.0 110.4 %reduce-scatter.3.cloned.1.call-start = ((), (), s32[]{:S(2)}) async-start(), calls=%async_computation.5 | async-start | bytes 1310720 | tf_op jit(solution)/shard_map/reduce_scatter | solution.py:36
  119.5 8.6 %copy-start.1 = (bf16[128,512]{1,0:T(8,128)(2,1)}, bf16[128,512]{1,0:T(8,128)(2,1)S(1)}, u32[]{:S(2)}) copy-start(bf16[128,512]{1,0:T(8,128)(2,1)S(1)} %get-tuple-element.7) | copy-start | bytes 393220
  144.6 116.0 %copy-start.10 = (bf16[1,2048,352]{1,2,0:T(8,128)(2,1)S(1)}, bf16[1,2048,352]{1,2,0:T(8,128)(2,1)}, u32[]{:S(2)}) copy-start(bf16[1,2048,352]{1,2,0:T(8,128)(2,1)} %param.21) | copy-start | bytes 4325380
  144.6 116.0 %all-to-all-start = ((bf16[64,16,2048]{2,1,0:T(8,128)(2,1)}), bf16[64,16,2048]{2,1,0:T(8,128)(2,1)}, u32[]{:S(2)}, u32[]{:S(2)}) async-start(bf16[64,16,2048]{2,1,0:T(8,128)(2,1)} %bitcast.50), calls=%async_computation.1 | async-start | bytes 8388608 | tf_op jit(solution)/shard_map/all_to_all | solution.py:58
  155.2 126.5 %all-gather.7.cloned.1.call-start = ((), (), s32[]{:S(2)}) async-start(), calls=%async_computation.6 | async-start | bytes 3194880 | tf_op jit(solution)/shard_map/all_gather | solution.py:84
  155.9 232.4 %all-gather.11.cloned.1.call-start = ((), (), s32[]{:S(2)}) async-start(), calls=%async_computation.8 | async-start | bytes 3194880 | tf_op jit(solution)/shard_map/all_gather | solution.py:90
  274.6 6.6 %copy-start.5 = (f32[128,6]{0,1:T(8,128)S(1)}, f32[128,6]{0,1:T(8,128)}, u32[]{:S(2)}) copy-start(f32[128,6]{0,1:T(8,128)} %param.25) | copy-start | bytes 9220
  274.6 109.6 %all-to-all-start.1 = ((bf16[64,16,2048]{2,1,0:T(8,128)(2,1)}), bf16[64,16,2048]{2,1,0:T(8,128)(2,1)}, u32[]{:S(2)}, u32[]{:S(2)}) async-start(bf16[64,16,2048]{2,1,0:T(8,128)(2,1)} %bitcast.51), calls=%async_computation.2 | async-start | bytes 8388608 | tf_op jit(solution)/shard_map/all_to_all | solution.py:70
  280.4 146.3 %all-gather.9.cloned.1.call-start = ((), (), s32[]{:S(2)}) async-start(), calls=%async_computation.7 | async-start | bytes 3194880 | tf_op jit(solution)/shard_map/all_gather | solution.py:85
  281.0 177.9 %reduce-scatter.5.cloned.1.call-start = ((), (), s32[]{:S(2)}) async-start(), calls=%async_computation.9 | async-start | bytes 1310720 | tf_op jit(solution)/shard_map/reduce_scatter | solution.py:91
  388.2 70.7 %copy-start.2 = (bf16[128,512]{1,0:T(8,128)(2,1)S(1)}, bf16[128,512]{1,0:T(8,128)(2,1)}, u32[]{:S(2)}) copy-start(bf16[128,512]{1,0:T(8,128)(2,1)} %copy-done.1) | copy-start | bytes 393220
  388.2 80.3 %copy-start.8 = (f32[512]{0:T(512)S(1)}, f32[512]{0:T(512)}, u32[]{:S(2)}) copy-start(f32[512]{0:T(512)} %param.27) | copy-start | bytes 6148
  460.0 9.3 %copy-start.3 = (bf16[128,512]{1,0:T(8,128)(2,1)}, bf16[128,512]{1,0:T(8,128)(2,1)S(1)}, u32[]{:S(2)}) copy-start(bf16[128,512]{1,0:T(8,128)(2,1)S(1)} %get-tuple-element.5) | copy-start | bytes 393220
Sparse Core Ops, SparseCore 0:
  10.8 79.1 all-gather.4
  93.6 24.6 reduce-scatter.2
  159.2 92.0 all-gather.6
  254.3 88.4 all-gather.10
  345.8 80.8 all-gather.8
  434.2 24.7 reduce-scatter.4
where the time goes:
time: 477 us; the launch traced here: 476 us
  waiting for transfers between devices  372 us (78%)
  matrix products  36 us (8%)
  blocking collectives  30.3 us (6%)
  starting transfers between devices  16.8 us (4%)
  between operations  14.3 us (3%)
  other arithmetic  5.93 us (1%)
    all_to_all x1, waiting for transfers between devices, local(): lax.all_to_all(outgoing.reshape(experts, capacity, model_width), 'dp', sp...  104 us
    all_to_all x1, waiting for transfers between devices, local(): lax.all_to_all(partial_out.reshape(experts, capacity, model_width), 'dp',...  98.6 us
    all_gather x1, waiting for transfers between devices, local(): lax.all_gather(out_weight, 'dp', axis=1, tiled=True)  82 us
    all_gather x1, waiting for transfers between devices, local(): lax.all_gather(shared_up, 'dp', axis=0, tiled=True)  38.4 us
    dot_general x6, matrix products, matmul(): return jnp.dot(left, right, preferred_element_type=jnp.float32)  32 us
    reduce_scatter x1, waiting for transfers between devices, local(): lax.psum_scatter(routed + shared_part, 'mp', scatter_dimension=1, tiled=T...  24.9 us
    reduce_scatter x1, waiting for transfers between devices, local(): lax.psum_scatter(partial_value, 'mp', scatter_dimension=1, tiled=True)  21.4 us
    all_gather x1, blocking collectives, local(): whole_rows = lax.all_gather(normed, 'mp', axis=1, tiled=True)  13.2 us
  transfers between devices with their start and end apart: 8, of which 6 were waited for; matrix products, arithmetic and copies ran while one was open for 5% of the time, Pallas kernels for 0%

commit v1 on v0

--- a/solution.py
+++ b/solution.py
@@ -2,6 +2,7 @@
 import jax.numpy as jnp
 from jax import lax
 from jax.sharding import PartitionSpec as P
+from jax.lax import all_to_all, axis_size
 
 D = 2048
 EPSILON = 1e-06
@@ -32,7 +33,14 @@
     experts = lax.axis_size("dp")
     capacity = min(tok_rows, 8 * tok_rows // experts)
     model_width = D
-    partial_value = matmul(attention, lax.all_gather(out_weight, "dp", axis=1, tiled=True))
+
+    def press_matrix_over_axis(x_local):
+        local_next = jnp.concatenate(
+            all_to_all(jnp.stack([x_local] * axis_size("dp"), axis=0), "dp", 0, 0), 1
+        )
+        return local_next
+
+    partial_value = matmul(attention, press_matrix_over_axis(out_weight))
     projected = lax.psum_scatter(partial_value, "mp", scatter_dimension=1, tiled=True)
     hidden = (residual.astype(jnp.float32) + projected).astype(jnp.bfloat16)
     hidden_float = hidden.astype(jnp.float32)

time: 477 us -> 456 us (0.956)
  waiting for transfers between devices: 372 us -> 287 us
  blocking collectives: 30.3 us -> 93.3 us
    all_gather x1 -> x0, waiting for transfers between devices: 82 us -> none  [local(): lax.all_gather(out_weight, 'dp', axis=1, tiled=True)]
    all_to_all x0 -> x1, blocking collectives: none -> 63.2 us  [press_matrix_over_axis(): all_to_all(jnp.stack([x_local] * axis_size('dp'), axis=0), 'dp', 0, 0)]
    all_gather x1, waiting for transfers between devices: 0.02 us -> 39.1 us  [local(): lax.all_gather(shared_down, 'dp', axis=1, tiled=True)]
    all_gather x1, waiting for transfers between devices: 38.4 us -> 0.03 us  [local(): lax.all_gather(shared_up, 'dp', axis=0, tiled=True)]
  transfers between devices with their start and end apart: 8 -> 7, of which waited for: 6 -> 5; matrix products, arithmetic and copies ran while one was open for 5% -> 6% of each run, Pallas kernels for 0% -> 0%
where the time goes in v1:
time: 456 us; the launch traced here: 455 us
  waiting for transfers between devices  287 us (63%)
  blocking collectives  93.3 us (20%)
  matrix products  34.3 us (8%)
  starting transfers between devices  16.9 us (4%)
  between operations  15.9 us (3%)
  other arithmetic  5.93 us (1%)
    all_to_all x1, waiting for transfers between devices, local(): lax.all_to_all(outgoing.reshape(experts, capacity, model_width), 'dp', sp...  104 us
    all_to_all x1, waiting for transfers between devices, local(): lax.all_to_all(partial_out.reshape(experts, capacity, model_width), 'dp',...  98.3 us
    all_to_all x1, blocking collectives, press_matrix_over_axis(): all_to_all(jnp.stack([x_local] * axis_size('dp'), axis=0), 'dp', 0, 0)  63.2 us
    all_gather x1, waiting for transfers between devices, local(): lax.all_gather(shared_down, 'dp', axis=1, tiled=True)  39.1 us
    dot_general x6, matrix products, matmul(): return jnp.dot(left, right, preferred_element_type=jnp.float32)  30.3 us
    reduce_scatter x1, waiting for transfers between devices, local(): lax.psum_scatter(routed + shared_part, 'mp', scatter_dimension=1, tiled=T...  24.8 us
    reduce_scatter x1, waiting for transfers between devices, local(): lax.psum_scatter(partial_value, 'mp', scatter_dimension=1, tiled=True)  19 us
    all_gather x1, blocking collectives, local(): whole_rows = lax.all_gather(normed, 'mp', axis=1, tiled=True)  13.2 us
  transfers between devices with their start and end apart: 7, of which 5 were waited for; matrix products, arithmetic and copies ran while one was open for 6% of the time, Pallas kernels for 0%

profile of v1, /device:TPU:8, one launch (start us, length us, event | category | flops | bytes accessed | tf_op | source)
XLA Modules:
  0.0 455.4 jit_solution(765891437915690407)
XLA Ops:
  8.0 0.0 copy-start
  8.0 0.0 copy-start.4
  8.0 0.0 reduce-scatter.3.cloned.1.call-start
  8.1 1.1 stack.2
  9.2 63.2 %all_to_all.15 = bf16[64,512,32]{1,2,0:T(8,128)(2,1)S(1)} all-to-all(bf16[64,512,32]{1,2,0:T(8,128)(2,1)S(1)} %stack.2), channel_id=1, replica_groups=mesh['dp'=64,'mp'=4] {'dp'}, dimensions={0} | all-to-all | bytes 4194304 | tf_op jit(solution)/shard_map/all_to_all | solution.py:39
  72.4 0.0 copy-start.7
  72.4 0.0 copy-start.10
  72.4 0.0 copy-done.4
  72.4 0.0 copy-start.8
  72.4 1.8 fusion.32
  74.2 0.0 reduce-scatter.3.cloned.1.call-update
  74.2 0.0 copy-done.7
  74.2 0.1 copy.22
  74.3 0.1 eq.43
  74.5 0.1 eq.39
  74.6 1.8 reduce-window.6
  76.4 0.3 slice_reduce_fusion
  76.7 0.0 copy-done.10
  76.7 0.1 select_reduce_fusion.1
  76.9 0.1 add.43
  77.0 0.1 copy.25
  77.1 0.5 fusion
  77.6 19.0 %reduce-scatter.3.cloned.1.call-done = f32[128,512]{1,0:T(8,128)} async-done(((f32[128,2048]{1,0:T(8,128)}), f32[128,512]{1,0:T(8,128)}) %reduce-scatter.3.cloned.1.call-update) | async-done | bytes 262160 | tf_op jit(solution)/shard_map/reduce_scatter | solution.py:44
  96.6 0.0 copy-done.5
  96.6 1.1 fusion.20
  97.7 8.5 %psum.14 = f32[128]{0:T(128)S(1)} all-reduce(f32[128]{0:T(128)S(1)} %get-tuple-element.6), channel_id=1, replica_groups=mesh['dp'=64,'mp'=4] {'mp'}, use_global_device_ids=true, to_apply=%region_8.9 | all-reduce | flops 128 | bytes 1024 | tf_op jit(solution)/shard_map/psum | solution.py:47
  106.2 0.0 copy-done.1
  106.2 0.0 copy-done.8
  106.2 0.1 fusion.22
  106.3 13.2 %all_gather.12 = bf16[128,2048]{1,0:T(8,128)(2,1)S(1)} all-gather(bf16[128,512]{1,0:T(8,128)(2,1)S(1)} %fusion.22), channel_id=1, replica_groups=mesh['dp'=64,'mp'=4] {'mp'}, dimensions={1}, use_global_device_ids=true | all-gather | bytes 655360 | tf_op jit(solution)/shard_map/all_gather | solution.py:51
  119.5 3.2 convolution_convert_fusion.1
  122.7 10.7 %all-to-all-start.1 = ((bf16[64,16,2048]{2,1,0:T(8,128)(2,1)}), bf16[64,16,2048]{2,1,0:T(8,128)(2,1)}, u32[]{:S(2)}, u32[]{:S(2)}) async-start(bf16[64,16,2048]{2,1,0:T(8,128)(2,1)} %bitcast.53), calls=%async_computation.2 | async-start | bytes 8388608 | tf_op jit(solution)/shard_map/all_to_all | solution.py:66
  133.4 0.0 all-gather.4.cloned.1.call-start
  133.5 0.5 all-gather.4.cloned.1.call-update
  134.0 0.0 all-gather.6.cloned.1.call-start
  134.0 0.5 all-gather.6.cloned.1.call-update
  134.6 104.2 %all-to-all-done.1 = bf16[64,16,2048]{2,1,0:T(8,128)(2,1)} async-done(((bf16[64,16,2048]{2,1,0:T(8,128)(2,1)}), bf16[64,16,2048]{2,1,0:T(8,128)(2,1)}, u32[]{:S(2)}, u32[]{:S(2)}) %all-to-all-start.1) | async-done | bytes 4194336 | tf_op jit(solution)/shard_map/all_to_all | solution.py:66
  238.7 0.0 copy-done.11
  238.7 5.1 %fusion.3 = f32[1024,352]{0,1:T(8,128)} fusion(bf16[1024,2048]{1,0:T(8,128)(2,1)} %bitcast.4, bf16[1,2048,352]{1,2,0:T(8,128)(2,1)S(1)} %copy-done.11), kind=kOutput, calls=%fused_computation.9 | convolution fusion | flops 1476395008 | bytes 7077888 | tf_op jit(solution)/shard_map/dot_general | solution.py:12
  243.9 0.0 copy-done
  243.9 8.9 %convolution_convert_fusion = bf16[1024,2048]{1,0:T(8,128)(2,1)} fusion(bf16[1,352,2048]{2,1,0:T(8,128)(2,1)S(1)} %copy-done, bf16[1024,2048]{1,0:T(8,128)(2,1)} %bitcast.4, bf16[1,2048,352]{1,2,0:T(8,128)(2,1)} %param.22, f32[1024,352]{0,1:T(8,128)} %fusion.3), kind=kOutput, calls=%fused_computation | convolution fusion | flops 2957049856 | bytes 12713984 | tf_op jit(solution)/shard_map/dot_general | solution.py:12
  252.8 5.8 %all-to-all-start.2 = ((bf16[64,16,2048]{2,1,0:T(8,128)(2,1)}), bf16[64,16,2048]{2,1,0:T(8,128)(2,1)}, u32[]{:S(2)}, u32[]{:S(2)}) async-start(bf16[64,16,2048]{2,1,0:T(8,128)(2,1)} %bitcast.55), calls=%async_computation.3 | async-start | bytes 8388608 | tf_op jit(solution)/shard_map/all_to_all | solution.py:78
  258.6 0.0 all-gather.8.cloned.1.call-start
  258.7 0.5 all-gather.8.cloned.1.call-update
  259.2 0.2 reduce-scatter.5.cloned.1.call-start
  259.4 0.0 copy-done.6
  259.4 0.4 select_reduce_fusion
  259.9 0.0 all-gather.4.cloned.1.call-done
  259.9 3.9 fusion.34
  263.8 98.3 %all-to-all-done.2 = bf16[64,16,2048]{2,1,0:T(8,128)(2,1)} async-done(((bf16[64,16,2048]{2,1,0:T(8,128)(2,1)}), bf16[64,16,2048]{2,1,0:T(8,128)(2,1)}, u32[]{:S(2)}, u32[]{:S(2)}) %all-to-all-start.2) | async-done | bytes 4194336 | tf_op jit(solution)/shard_map/all_to_all | solution.py:78
  362.2 4.0 fusion.33
  366.2 0.0 copy-start.2
  366.2 0.0 copy-start.9
  366.2 0.0 all-gather.6.cloned.1.call-done
  366.2 39.1 %all-gather.8.cloned.1.call-done = bf16[704,2048]{0,1:T(8,128)(2,1)} async-done(((bf16[704,32]{0,1:T(8,128)(2,1)}), bf16[704,2048]{0,1:T(8,128)(2,1)}) %all-gather.8.cloned.1.call-update) | async-done | bytes 2883600 | tf_op jit(solution)/shard_map/all_gather | solution.py:98
  405.3 7.3 %convolution_add_fusion = f32[128,2048]{1,0:T(8,128)} fusion(f32[128,2048]{1,0:T(8,128)S(1)} %fusion.33, bf16[704,2048]{0,1:T(8,128)(2,1)} %all-gather.8.cloned.1.call-done, bf16[128,2048]{1,0:T(8,128)(2,1)S(1)} %all_gather.12, bf16[2048,704]{1,0:T(8,128)(2,1)} %all-gather.6.cloned.1.call-done, f32[128,704]{0,1:T(8,128)} %fusion.34), kind=kOutput, calls=%fused_computation.5 | convolution fusion | flops 739000320 | bytes 8749056 | tf_op jit(solution)/shard_map/dot_general | solution.py:12
  412.7 0.0 reduce-scatter.5.cloned.1.call-update
  412.7 24.8 %reduce-scatter.5.cloned.1.call-done = f32[128,512]{1,0:T(8,128)} async-done(((f32[128,2048]{1,0:T(8,128)}), f32[128,512]{1,0:T(8,128)}) %reduce-scatter.5.cloned.1.call-update) | async-done | bytes 262160 | tf_op jit(solution)/shard_map/reduce_scatter | solution.py:99
  437.4 0.0 copy-done.2
  437.5 1.1 fusion.17
  438.5 8.5 %psum.15 = f32[128]{0:T(128)S(1)} all-reduce(f32[128]{0:T(128)S(1)} %get-tuple-element.4), channel_id=1, replica_groups=mesh['dp'=64,'mp'=4] {'mp'}, use_global_device_ids=true, to_apply=%region_11.12 | all-reduce | flops 128 | bytes 1024 | tf_op jit(solution)/shard_map/psum | solution.py:102
  447.0 0.0 copy-done.9
  447.0 0.8 fusion.19
  447.8 0.0 copy-done.3
  (10 shorter events, 0.1 us)
Async XLA Ops:
  8.0 235.9 %copy-start = (bf16[1,352,2048]{2,1,0:T(8,128)(2,1)S(1)}, bf16[1,352,2048]{2,1,0:T(8,128)(2,1)}, u32[]{:S(2)}) copy-start(bf16[1,352,2048]{2,1,0:T(8,128)(2,1)} %param.23) | copy-start | bytes 4325380
  8.0 64.4 %copy-start.4 = (bf16[128,512]{1,0:T(8,128)(2,1)S(1)}, bf16[128,512]{1,0:T(8,128)(2,1)}, u32[]{:S(2)}) copy-start(bf16[128,512]{1,0:T(8,128)(2,1)} %param.14) | copy-start | bytes 393220
  8.0 88.6 %reduce-scatter.3.cloned.1.call-start = ((), (), s32[]{:S(2)}) async-start(), calls=%async_computation.5 | async-start | bytes 1310720 | tf_op jit(solution)/shard_map/reduce_scatter | solution.py:44
  72.4 1.8 copy-start.7
  72.4 4.4 copy-start.10
  72.4 24.2 %copy-start.5 = (bf16[128,512]{1,0:T(8,128)(2,1)S(1)}, bf16[128,512]{1,0:T(8,128)(2,1)}, u32[]{:S(2)}) copy-start(bf16[128,512]{1,0:T(8,128)(2,1)} %param.15) | copy-start | bytes 393220
  72.4 33.9 %copy-start.8 = (f32[512]{0:T(512)S(1)}, f32[512]{0:T(512)}, u32[]{:S(2)}) copy-start(f32[512]{0:T(512)} %param.17) | copy-start | bytes 6148
  97.7 8.6 %copy-start.1 = (bf16[128,512]{1,0:T(8,128)(2,1)}, bf16[128,512]{1,0:T(8,128)(2,1)S(1)}, u32[]{:S(2)}) copy-start(bf16[128,512]{1,0:T(8,128)(2,1)S(1)} %get-tuple-element.7) | copy-start | bytes 393220
  122.7 116.0 %copy-start.11 = (bf16[1,2048,352]{1,2,0:T(8,128)(2,1)S(1)}, bf16[1,2048,352]{1,2,0:T(8,128)(2,1)}, u32[]{:S(2)}) copy-start(bf16[1,2048,352]{1,2,0:T(8,128)(2,1)} %param.21) | copy-start | bytes 4325380
  122.7 116.0 %all-to-all-start.1 = ((bf16[64,16,2048]{2,1,0:T(8,128)(2,1)}), bf16[64,16,2048]{2,1,0:T(8,128)(2,1)}, u32[]{:S(2)}, u32[]{:S(2)}) async-start(bf16[64,16,2048]{2,1,0:T(8,128)(2,1)} %bitcast.53), calls=%async_computation.2 | async-start | bytes 8388608 | tf_op jit(solution)/shard_map/all_to_all | solution.py:66
  133.4 126.5 %all-gather.4.cloned.1.call-start = ((), (), s32[]{:S(2)}) async-start(), calls=%async_computation.6 | async-start | bytes 3194880 | tf_op jit(solution)/shard_map/all_gather | solution.py:92
  134.0 232.3 %all-gather.6.cloned.1.call-start = ((), (), s32[]{:S(2)}) async-start(), calls=%async_computation.7 | async-start | bytes 3194880 | tf_op jit(solution)/shard_map/all_gather | solution.py:93
  252.8 6.6 %copy-start.6 = (f32[128,6]{0,1:T(8,128)S(1)}, f32[128,6]{0,1:T(8,128)}, u32[]{:S(2)}) copy-start(f32[128,6]{0,1:T(8,128)} %param.25) | copy-start | bytes 9220
  252.8 109.4 %all-to-all-start.2 = ((bf16[64,16,2048]{2,1,0:T(8,128)(2,1)}), bf16[64,16,2048]{2,1,0:T(8,128)(2,1)}, u32[]{:S(2)}, u32[]{:S(2)}) async-start(bf16[64,16,2048]{2,1,0:T(8,128)(2,1)} %bitcast.55), calls=%async_computation.3 | async-start | bytes 8388608 | tf_op jit(solution)/shard_map/all_to_all | solution.py:78
  258.6 146.7 %all-gather.8.cloned.1.call-start = ((), (), s32[]{:S(2)}) async-start(), calls=%async_computation.8 | async-start | bytes 3194880 | tf_op jit(solution)/shard_map/all_gather | solution.py:98
  259.2 178.3 %reduce-scatter.5.cloned.1.call-start = ((), (), s32[]{:S(2)}) async-start(), calls=%async_computation.9 | async-start | bytes 1310720 | tf_op jit(solution)/shard_map/reduce_scatter | solution.py:99
  366.2 71.3 %copy-start.2 = (bf16[128,512]{1,0:T(8,128)(2,1)S(1)}, bf16[128,512]{1,0:T(8,128)(2,1)}, u32[]{:S(2)}) copy-start(bf16[128,512]{1,0:T(8,128)(2,1)} %copy-done.1) | copy-start | bytes 393220
  366.2 80.8 %copy-start.9 = (f32[512]{0:T(512)S(1)}, f32[512]{0:T(512)}, u32[]{:S(2)}) copy-start(f32[512]{0:T(512)} %param.27) | copy-start | bytes 6148
  438.5 9.3 %copy-start.3 = (bf16[128,512]{1,0:T(8,128)(2,1)}, bf16[128,512]{1,0:T(8,128)(2,1)S(1)}, u32[]{:S(2)}) copy-start(bf16[128,512]{1,0:T(8,128)(2,1)S(1)} %get-tuple-element.5) | copy-start | bytes 393220
Sparse Core Ops, SparseCore 0:
  74.3 22.2 reduce-scatter.2
  412.8 24.6 reduce-scatter.4
Sparse Core Ops, SparseCore 1:
  137.0 92.9 all-gather.3
  232.9 87.9 all-gather.5
  323.9 81.4 all-gather.7
